TPU v7x, 32 devices: a whole 2x2x4 slice. The times are simulated.
32 devices in a mesh: freq: 2 (over x), atom: 16 (over z, y, core).
Axes of the slice: x: 2, y: 2, z: 4, core: 2. Of those that a mesh axis runs over, the one named last changes fastest.
Arguments:
- ham_diag: float32 [2, 128, 128], replicated
- ham_coup: float32 [1, 128, 128], replicated, may hold values from -0.25 to 0.25
- neighbors: int32 [256, 64], replicated, may hold values from 0 to 127, as said below
- pair_count: int32 [256], replicated, may hold values from 16 to 64
- shifts: int32 [8], replicated, may hold values from 1 to 16
- g_pairs: float32 [2, 32, 16384], P(None, ('freq', 'atom')), may hold values from -3 to 3
- emit_coup: float32 [2, 8, 16384], replicated, may hold values from -0.09375 to 0.09375
- absorb_coup: float32 [2, 8, 16384], replicated, may hold values from -0.09375 to 0.09375
Outputs:
- green: float32 [2, 32, 2, 128, 128], P(None, ('freq', 'atom'))
Inputs may be any that keep to these rules, and one draw needn't show every extreme that they name: `neighbors`: entry 0 of each row is the atom's own index within its slab (atom index modulo 128); the entries of a row are distinct.
All inputs are finite; a program needn't handle non-finite values.
Results may differ from a plain program's by a relative error of at most 0.0001.
Values sent between devices are 32-bit elements; how exact they have to be, the bound alone decides.
No kernel may reach another device: no remote copies, remote signals or barrier semaphores. Data moves between devices by JAX's collectives and lax.ppermute only.
A program may use at most 128 MiB of HBM per device.

v0:
```python
import jax
import jax.numpy as jnp
from jax import lax
from jax.sharding import PartitionSpec as P

ORB = 128
SLABS = 2
NBR = 64
MODES = 8
HALO = 16
INV_STEPS = 22
BROADEN = 0.8
ENERGY_LOW = -2.5
ENERGY_SPAN = 5.0


def with_halo(cells, sides, width):
    for axis, dim in sides:
        count = lax.axis_size(axis)
        ends = count - 1
        head = lax.slice_in_dim(cells, 0, width, axis=dim)
        tail = lax.slice_in_dim(cells, cells.shape[dim] - width, cells.shape[dim], axis=dim)
        cells = jnp.concatenate(
            [
                lax.ppermute(tail, axis, [(i, (i + 1) % count) for i in range(ends)]),
                cells,
                lax.ppermute(head, axis, [((i + 1) % count, i) for i in range(ends)]),
            ],
            axis=dim,
        )
    return cells


def matmul(left, right):
    return jnp.dot(left, right, precision=lax.Precision.HIGHEST, preferred_element_type=jnp.float32)


def complex_product(left, right):
    first = matmul(left[0], right[0])
    second = matmul(left[1], right[1])
    third = matmul(left[0] + left[1], right[0] + right[1])
    return (first - second, third - first - second)


def sandwich(outer_left, inner, outer_right):
    return (
        matmul(matmul(outer_left, inner[0]), outer_right),
        matmul(matmul(outer_left, inner[1]), outer_right),
    )


def invert(real_part, imag_part):
    order = real_part.shape[0]
    unit_matrix = jnp.eye(order, dtype=real_part.dtype)
    scale = 1.0 / (jnp.sum(real_part * real_part) + jnp.sum(imag_part * imag_part))
    start = (real_part.T * scale, -imag_part.T * scale)

    def newton_step(index, current):
        product = complex_product((real_part, imag_part), current)
        residue = (2.0 * unit_matrix - product[0], -product[1])
        return complex_product(current, residue)

    return lax.fori_loop(0, INV_STEPS, newton_step, start)


def slab_green(sigma_blocks, energy, ham_diag, ham_coup):
    slabs = ham_diag.shape[0]
    order = ham_diag.shape[1]
    unit_matrix = jnp.eye(order, dtype=ham_diag.dtype)
    diag_real = [
        energy * unit_matrix - ham_diag[slab_index] - sigma_blocks[0, slab_index]
        for slab_index in range(slabs)
    ]
    diag_imag = [BROADEN * unit_matrix - sigma_blocks[1, slab_index] for slab_index in range(slabs)]
    right_parts = [None] * slabs
    right_parts[slabs - 1] = invert(diag_real[slabs - 1], diag_imag[slabs - 1])
    slab_index = 0
    coupling = ham_coup[slab_index]
    folded = sandwich(coupling, right_parts[slab_index + 1], coupling.T)
    right_parts[slab_index] = invert(
        diag_real[slab_index] - folded[0], diag_imag[slab_index] - folded[1]
    )
    blocks = [right_parts[0]]
    slab_index = 1
    coupling = ham_coup[slab_index - 1]
    carried = sandwich(coupling.T, blocks[-1], coupling)
    own_part = right_parts[slab_index]
    update = complex_product(complex_product(own_part, carried), own_part)
    blocks.append((own_part[0] + update[0], own_part[1] + update[1]))
    return jnp.stack(
        [jnp.stack([entry[0] for entry in blocks]), jnp.stack([entry[1] for entry in blocks])]
    )


def sigma_blocks_of(sigma_pairs, neighbors, live):
    values = sigma_pairs.reshape(2, SLABS, ORB, NBR) * live
    slab_ids = jnp.broadcast_to(
        jnp.arange(SLABS, dtype=jnp.int32)[:, None, None], (SLABS, ORB, NBR)
    )
    row_ids = jnp.broadcast_to(jnp.arange(ORB, dtype=jnp.int32)[None, :, None], (SLABS, ORB, NBR))
    columns = neighbors.reshape(SLABS, ORB, NBR)
    empty = jnp.zeros((2, SLABS, ORB, ORB), sigma_pairs.dtype)
    return empty.at[:, slab_ids, row_ids, columns].add(values)


def convolve(source, base, length, shifts, emit_coup, absorb_coup):
    width = source.shape[2]
    real_sum = jnp.zeros((length, width), source.dtype)
    imag_sum = jnp.zeros((length, width), source.dtype)
    for mode_index in range(MODES):
        shift_now = shifts[mode_index]
        below = lax.dynamic_slice_in_dim(source, base - shift_now, length, 1)
        above = lax.dynamic_slice_in_dim(source, base + shift_now, length, 1)
        emit_real = emit_coup[0, mode_index][None, :]
        emit_imag = emit_coup[1, mode_index][None, :]
        absorb_real = absorb_coup[0, mode_index][None, :]
        absorb_imag = absorb_coup[1, mode_index][None, :]
        real_sum = (
            real_sum
            + emit_real * below[0]
            - emit_imag * below[1]
            + absorb_real * above[0]
            - absorb_imag * above[1]
        )
        imag_sum = (
            imag_sum
            + emit_real * below[1]
            + emit_imag * below[0]
            + absorb_real * above[1]
            + absorb_imag * above[0]
        )
    return jnp.stack([real_sum, imag_sum])


def on_device(ham_diag, ham_coup, neighbors, pair_count, shifts, g_pairs, emit_coup, absorb_coup):
    e_dev = g_pairs.shape[1]
    atom_count = lax.axis_size("atom")
    group = e_dev * atom_count
    energy_total = group * lax.axis_size("freq")
    freq_index = lax.axis_index("freq")
    atom_index = lax.axis_index("atom")
    live = (
        (jnp.arange(NBR, dtype=jnp.int32)[None, :] < pair_count[:, None])
        .astype(jnp.float32)
        .reshape(SLABS, ORB, NBR)
    )
    first_energy = (freq_index * atom_count + atom_index) * e_dev

    def solve_one(sigma_pairs, energy):
        return slab_green(sigma_blocks_of(sigma_pairs, neighbors, live), energy, ham_diag, ham_coup)

    owned = lax.all_to_all(g_pairs, "atom", split_axis=2, concat_axis=1, tiled=True)
    owned_width = owned.shape[2]
    own_emit = lax.dynamic_slice_in_dim(emit_coup, atom_index * owned_width, owned_width, 2)
    own_absorb = lax.dynamic_slice_in_dim(absorb_coup, atom_index * owned_width, owned_width, 2)
    source = with_halo(owned, (("freq", 1),), HALO)
    sigma = convolve(source, HALO, group, shifts, own_emit, own_absorb)
    returned = lax.all_to_all(sigma, "atom", split_axis=1, concat_axis=2, tiled=True)

    def single(pieces):
        return solve_one(pieces[0], pieces[1])

    positions = (first_energy + jnp.arange(e_dev, dtype=jnp.int32)).astype(jnp.float32)
    solved = lax.map(
        single, (jnp.moveaxis(returned, 1, 0), ENERGY_LOW + ENERGY_SPAN * positions / energy_total)
    )
    return jnp.moveaxis(solved, 0, 1)


def solution(mesh):
    return jax.shard_map(
        on_device,
        mesh=mesh,
        in_specs=(P(), P(), P(), P(), P(), P(None, ("freq", "atom"), None), P(), P()),
        out_specs=P(None, ("freq", "atom"), None, None, None),
        check_vma=False,
    )
```

profile of v0, /device:TPU:0, one launch (start us, length us, event | category | flops | bytes accessed | tf_op | source)
XLA Modules:
  0.0 409.6 jit_solution(11434350478482396900)
XLA Ops:
  0.0 14.7 %copy.80 = f32[2,1,16384]{0,1,2:T(1,128)} copy(f32[2,1,16384]{2,1,0:T(1,128)} %param.17) | data formatting | bytes 262144 | tf_op args[5]
  15.2 74.4 %reduce.4 = f32[16384,2]{1,0:T(8,128)} reduce(f32[16384,1,2]{2,1,0:T(1,128)} %bitcast.233, f32[]{:T(128)} %broadcast.412), dimensions={1}, to_apply=%bitcast.153.reduce_sub_computation | reduce | bytes 262148
  89.6 8.3 %reshape.561 = f32[16,1,2048]{2,1,0:T(1,128)} reshape(f32[16384,2]{1,0:T(8,128)} %reduce.4) | data formatting | bytes 262144
  97.9 7.4 %all-to-all-start = ((f32[16,1,2048]{2,1,0:T(1,128)}), f32[16,1,2048]{2,1,0:T(1,128)S(1)}, u32[]{:S(2)}, u32[]{:S(2)}) async-start(f32[16,1,2048]{2,1,0:T(1,128)} %reshape.561), calls=%async_computation | async-start | bytes 262144 | tf_op jit(solution)/shard_map/all_to_all | solution.py:152
  126.2 2.0 constant_dynamic-slice_fusion.1
  129.4 14.7 %reshape.562 = f32[16384,1,2]{2,1,0:T(1,128)} reshape(f32[16,2048]{1,0:T(8,128)S(1)} %reduce.5) | data formatting | bytes 262144
  144.2 5.2 %copy.95 = f32[2,16,1024]{2,1,0:T(8,128)S(1)} copy(f32[2,16,1024]{0,2,1:T(8,128)} %bitcast.234) | data formatting | bytes 262144 | tf_op jit(solution)/shard_map/all_to_all | solution.py:152
  149.4 1.3 collective-permute-start.1
  150.7 4.6 %collective-permute-start = (f32[2,16,1024]{2,1,0:T(8,128)S(1)}, f32[2,16,1024]{2,1,0:T(8,128)S(1)}, u32[]{:S(2)}, u32[]{:S(2)}) collective-permute-start(f32[2,16,1024]{2,1,0:T(8,128)S(1)} %copy.95), channel_id=1, source_target_pairs={{0,16},{1,17},{2,18},{3,19},{4,20},{5,21},{6,22},{7,23},{8,24},{9,... | collective-permute-start | bytes 393224 | tf_op jit(solution)/shard_map/ppermute | solution.py:25
  155.5 1.7 collective-permute-done.1
  157.2 1.2 collective-permute-done
  160.4 5.8 %all-to-all-start.1 = ((f32[2,16,1024]{2,0,1:T(2,128)}), f32[2,16,1024]{2,0,1:T(2,128)S(1)}, u32[]{:S(2)}, u32[]{:S(2)}) async-start(f32[2,16,1024]{2,0,1:T(2,128)} %copy.82), calls=%async_computation.1 | async-start | bytes 262144 | tf_op jit(solution)/shard_map/all_to_all | solution.py:158
  166.5 7.5 %all-to-all-done.1 = f32[2,16,1024]{2,0,1:T(2,128)S(1)} async-done(((f32[2,16,1024]{2,0,1:T(2,128)}), f32[2,16,1024]{2,0,1:T(2,128)S(1)}, u32[]{:S(2)}, u32[]{:S(2)}) %all-to-all-start.1) | async-done | bytes 131104 | tf_op jit(solution)/shard_map/all_to_all | solution.py:158
  174.2 4.8 %copy.96 = f32[2,128,64,2]{3,2,1,0:T(8,128)} copy(f32[2,128,64,2]{2,1,0,3:T(8,128)S(1)} %multiply_bitcast_fusion) | data formatting | bytes 262144 | tf_op jit(solution)/shard_map/while/body/eval_jaxpr/mul | solution.py:96
  179.0 94.4 %scatter_custom_fusion = f32[2,32768]{0,1:T(8,128)} fusion(s32[16384]{0:T(1024)S(1)} %reshape.553, f32[16384,2]{1,0:T(8,128)} %bitcast.235, f32[]{:T(128)} %constant.119.clone.1), kind=kCustom, calls=%fused_computation.37 | custom fusion | flops 32768 | bytes 262656
  273.4 27.8 %fusion.60 = (f32[1,1,128,128]{0,3,2,1:T(8,128)}, f32[1,1,128,128]{0,3,2,1:T(8,128)}, f32[1,1,128,128]{0,3,2,1:T(8,128)}, f32[1,1,128,128]{0,3,2,1:T(8,128)}) fusion(f32[2,2,128,128]{0,3,2,1:T(8,128)} %bitcast.232), kind=kLoop, calls=%fused_computation.120 | loop fusion | bytes 524288 | tf_op jit(solution)/shard_map/while/body/eval_jaxpr/slice | solution.py:74
  301.2 5.2 %copy.100 = f32[1,1,128,128]{3,2,1,0:T(8,128)S(1)} copy(f32[1,1,128,128]{0,3,2,1:T(8,128)} %get-tuple-element.218) | data formatting | bytes 131072
  306.4 5.2 %copy.99 = f32[1,1,128,128]{3,2,1,0:T(8,128)S(1)} copy(f32[1,1,128,128]{0,3,2,1:T(8,128)} %get-tuple-element.219) | data formatting | bytes 131072
  314.4 38.5 %while.40 = (s32[]{:T(128)}, f32[128,128]{0,1:T(8,128)S(1)}, f32[128,128]{0,1:T(8,128)S(1)}, f32[128,128]{1,0:T(8,128)S(1)}, f32[128,128]{1,0:T(8,128)S(1)}, /*index=5*/f32[128,128]{1,0:T(8,128)S(1)}, s32[]{:T(128)}) while((s32[]{:T(128)}, f32[128,128]{0,1:T(8,128)S(1)}, f32[128,128]{0,1:T(8,128)S(1)}, f32[128,128]{1,0:T(8,128)S(1)}, ...), condition=%wide.region_4.5_spmd.clone, body=%wide.region_3.4_spmd.clone.sunk | while | flops 151273472 | bytes 2162765 | solution.py:63
  353.7 5.2 %copy.101 = f32[1,1,128,128]{3,2,1,0:T(8,128)S(1)} copy(f32[1,1,128,128]{0,3,2,1:T(8,128)} %get-tuple-element.217) | data formatting | bytes 131072
  358.9 5.2 %copy.98 = f32[1,1,128,128]{3,2,1,0:T(8,128)S(1)} copy(f32[1,1,128,128]{0,3,2,1:T(8,128)} %get-tuple-element.220) | data formatting | bytes 131072
  364.1 1.0 multiply_reduce_fusion.1
  365.1 0.9 multiply_reduce_fusion.2
  367.4 38.5 %while.41 = (s32[]{:T(128)}, f32[128,128]{0,1:T(8,128)S(1)}, f32[128,128]{0,1:T(8,128)S(1)}, f32[128,128]{1,0:T(8,128)S(1)}, f32[128,128]{1,0:T(8,128)S(1)}, /*index=5*/f32[128,128]{1,0:T(8,128)S(1)}, s32[]{:T(128)}) while((s32[]{:T(128)}, f32[128,128]{0,1:T(8,128)S(1)}, f32[128,128]{0,1:T(8,128)S(1)}, f32[128,128]{1,0:T(8,128)S(1)}, ...), condition=%wide.region_8.9_spmd.clone, body=%wide.region_7.8_spmd.clone.sunk | while | flops 151273472 | bytes 2162765 | solution.py:63
  (413 shorter events, 85.4 us)
Async XLA Ops:
  0.0 353.0 %copy-start = (f32[1,128,128]{2,1,0:T(8,128)S(1)}, f32[1,128,128]{2,1,0:T(8,128)}, u32[]{:S(2)}) copy-start(f32[1,128,128]{2,1,0:T(8,128)} %param.13) | copy-start | bytes 196612
  89.6 15.7 %copy-start.3 = (s32[8]{0:T(128)S(1)}, s32[8]{0:T(128)}, u32[]{:S(2)}) copy-start(s32[8]{0:T(128)} %param.16) | copy-start | bytes 100
  89.6 36.4 %copy-start.2 = (s32[256,64]{0,1:T(8,128)S(1)}, s32[256,64]{0,1:T(8,128)}, u32[]{:S(2)}) copy-start(s32[256,64]{0,1:T(8,128)} %param.14) | copy-start | bytes 196612
  89.6 38.7 %copy-start.6 = (s32[3]{0:T(128)S(1)}, s32[3]{0:T(128)}, u32[]{:S(2)}) copy-start(s32[3]{0:T(128)} %constant.131) | copy-start | bytes 40
  97.9 30.7 %all-to-all-start = ((f32[16,1,2048]{2,1,0:T(1,128)}), f32[16,1,2048]{2,1,0:T(1,128)S(1)}, u32[]{:S(2)}, u32[]{:S(2)}) async-start(f32[16,1,2048]{2,1,0:T(1,128)} %reshape.561), calls=%async_computation | async-start | bytes 262144 | tf_op jit(solution)/shard_map/all_to_all | solution.py:152
  129.4 25.9 %copy-start.5 = (s32[3]{0:T(128)S(1)}, s32[3]{0:T(128)}, u32[]{:S(2)}) copy-start(s32[3]{0:T(128)} %constant.128) | copy-start | bytes 40
  144.2 22.2 %copy-start.4 = (s32[256]{0:T(256)S(1)}, s32[256]{0:T(256)}, u32[]{:S(2)}) copy-start(s32[256]{0:T(256)} %param.15) | copy-start | bytes 3076
  149.4 7.7 %collective-permute-start.1 = (f32[2,16,1024]{2,1,0:T(8,128)S(1)}, f32[2,16,1024]{2,1,0:T(8,128)S(1)}, u32[]{:S(2)}, u32[]{:S(2)}) collective-permute-start(f32[2,16,1024]{2,1,0:T(8,128)S(1)} %copy.95), channel_id=1, source_target_pairs={{16,0},{17,1},{18,2},{19,3},{20,4},{21,5},{22,6},{23,7},{24,8},{25... | collective-permute-start | bytes 393224 | tf_op jit(solution)/shard_map/ppermute | solution.py:27
  150.7 7.6 %collective-permute-start = (f32[2,16,1024]{2,1,0:T(8,128)S(1)}, f32[2,16,1024]{2,1,0:T(8,128)S(1)}, u32[]{:S(2)}, u32[]{:S(2)}) collective-permute-start(f32[2,16,1024]{2,1,0:T(8,128)S(1)} %copy.95), channel_id=1, source_target_pairs={{0,16},{1,17},{2,18},{3,19},{4,20},{5,21},{6,22},{7,23},{8,24},{9,... | collective-permute-start | bytes 393224 | tf_op jit(solution)/shard_map/ppermute | solution.py:25
  160.4 13.7 %all-to-all-start.1 = ((f32[2,16,1024]{2,0,1:T(2,128)}), f32[2,16,1024]{2,0,1:T(2,128)S(1)}, u32[]{:S(2)}, u32[]{:S(2)}) async-start(f32[2,16,1024]{2,0,1:T(2,128)} %copy.82), calls=%async_computation.1 | async-start | bytes 262144 | tf_op jit(solution)/shard_map/all_to_all | solution.py:158
  301.2 10.5 %copy-start.1 = (f32[2,128,128]{2,1,0:T(8,128)S(1)}, f32[2,128,128]{2,1,0:T(8,128)}, u32[]{:S(2)}) copy-start(f32[2,128,128]{2,1,0:T(8,128)} %param.12) | copy-start | bytes 393220
where the time goes:
time: 412 us; the launch traced here: 410 us
  other arithmetic  174 us (42%)
  local copies, waits for them, and re-layouts  102 us (25%)
  matrix products  79.1 us (19%)
  between operations  23.3 us (6%)
  starting transfers between devices  19 us (5%)
  waiting for transfers between devices  10.4 us (3%)
    unnamed x5, other arithmetic  169 us
    dot_general x278, matrix products, matmul(): jnp.dot(left, right, precision=lax.Precision.HIGHEST, preferred_element_t...  79.1 us
    unnamed x24, local copies, waits for them, and re-layouts  59.3 us
    slice x1, local copies, waits for them, and re-layouts, slab_green(): sigma_blocks[1, slab_index]  27.8 us
  transfers between devices with their start and end apart: 4, of which 3 were waited for; matrix products, arithmetic and copies ran while one was open for 1% of the time, Pallas kernels for 0%

commit v1 on v0

--- a/solution.py
+++ b/solution.py
@@ -149,7 +149,10 @@
     def solve_one(sigma_pairs, energy):
         return slab_green(sigma_blocks_of(sigma_pairs, neighbors, live), energy, ham_diag, ham_coup)
 
-    owned = lax.all_to_all(g_pairs, "atom", split_axis=2, concat_axis=1, tiled=True)
+    owned = jnp.concatenate(
+        lax.all_to_all(jnp.stack(jnp.split(g_pairs, lax.axis_size("atom"), axis=2)), "atom", 0, 0),
+        axis=1,
+    )
     owned_width = owned.shape[2]
     own_emit = lax.dynamic_slice_in_dim(emit_coup, atom_index * owned_width, owned_width, 2)
     own_absorb = lax.dynamic_slice_in_dim(absorb_coup, atom_index * owned_width, owned_width, 2)

time: 412 us -> 304 us (0.74)
  other arithmetic: 174 us -> 99.7 us
  local copies, waits for them, and re-layouts: 102 us -> 70.9 us
    unnamed x5 -> x4, other arithmetic: 169 us -> 96.2 us
    unnamed x24 -> x27, local copies, waits for them, and re-layouts: 59.3 us -> 30.1 us
    all_to_all x1, local copies, waits for them, and re-layouts: 5.23 us -> 0.05 us  [on_device(): lax.all_to_all(jnp.stack(jnp.split(g_pairs, lax.axis_size('atom'), axis=2...]
  transfers between devices with their start and end apart: 4 -> 4, of which waited for: 3 -> 3; matrix products, arithmetic and copies ran while one was open for 1% -> 2% of each run, Pallas kernels for 0% -> 0%
where the time goes in v1:
time: 304 us; the launch traced here: 303 us
  other arithmetic  99.7 us (33%)
  matrix products  79 us (26%)
  local copies, waits for them, and re-layouts  70.9 us (23%)
  between operations  23 us (8%)
  starting transfers between devices  18.8 us (6%)
  waiting for transfers between devices  9.6 us (3%)
    unnamed x4, other arithmetic  96.2 us
    dot_general x278, matrix products, matmul(): jnp.dot(left, right, precision=lax.Precision.HIGHEST, preferred_element_t...  79 us
    unnamed x27, local copies, waits for them, and re-layouts  30.1 us
    slice x1, local copies, waits for them, and re-layouts, slab_green(): sigma_blocks[1, slab_index]  27.8 us
    all_to_all x1, waiting for transfers between devices, on_device(): lax.all_to_all(sigma, 'atom', split_axis=1, concat_axis=2, tiled=True)  7.52 us
    all_to_all x1, starting transfers between devices, on_device(): lax.all_to_all(jnp.stack(jnp.split(g_pairs, lax.axis_size('atom'), axis=2...  7.41 us
  transfers between devices with their start and end apart: 4, of which 3 were waited for; matrix products, arithmetic and copies ran while one was open for 2% of the time, Pallas kernels for 0%

profile of v1, /device:TPU:0, one launch (start us, length us, event | category | flops | bytes accessed | tf_op | source)
XLA Modules:
  0.0 303.3 jit_solution(3694903082982405307)
XLA Ops:
  0.0 0.9 fusion.61
  10.5 7.4 %all-to-all-start = ((f32[16,2,1,1024]{3,1,2,0:T(2,128)}), f32[16,2,1,1024]{3,1,2,0:T(2,128)S(1)}, u32[]{:S(2)}, u32[]{:S(2)}) async-start(f32[16,2,1,1024]{3,1,2,0:T(2,128)} %constant_dynamic-update-slice_fusion), calls=%async_computation | async-start | bytes 262144 | tf_op jit(solution)/shard_map/all_to_all | solution.py:153
  18.0 1.6 fusion.63
  39.6 0.9 reshape.550
  40.7 2.2 constant_dynamic-slice_fusion.1
  43.0 0.9 and_reduce_fusion
  44.0 1.3 collective-permute-start.1
  45.3 4.6 %collective-permute-start = (f32[2,16,1024]{2,1,0:T(8,128)S(1)}, f32[2,16,1024]{2,1,0:T(8,128)S(1)}, u32[]{:S(2)}, u32[]{:S(2)}) collective-permute-start(f32[2,16,1024]{2,1,0:T(8,128)S(1)} %bitcast.301), channel_id=1, source_target_pairs={{0,16},{1,17},{2,18},{3,19},{4,20},{5,21},{6,22},{7,23},{8,24},{9,... | collective-permute-start | bytes 393224 | tf_op jit(solution)/shard_map/ppermute | solution.py:25
  49.8 0.9 multiply_reduce_fusion
  50.7 0.9 collective-permute-done.1
  51.6 1.2 collective-permute-done
  54.8 5.5 %all-to-all-start.1 = ((f32[2,16,1024]{2,0,1:T(2,128)}), f32[2,16,1024]{2,0,1:T(2,128)S(1)}, u32[]{:S(2)}, u32[]{:S(2)}) async-start(f32[2,16,1024]{2,0,1:T(2,128)} %copy.90), calls=%async_computation.1 | async-start | bytes 262144 | tf_op jit(solution)/shard_map/all_to_all | solution.py:161
  60.7 7.5 %all-to-all-done.1 = f32[2,16,1024]{2,0,1:T(2,128)S(1)} async-done(((f32[2,16,1024]{2,0,1:T(2,128)}), f32[2,16,1024]{2,0,1:T(2,128)S(1)}, u32[]{:S(2)}, u32[]{:S(2)}) %all-to-all-start.1) | async-done | bytes 131104 | tf_op jit(solution)/shard_map/all_to_all | solution.py:161
  68.4 4.8 %copy.103 = f32[2,128,64,2]{3,2,1,0:T(8,128)} copy(f32[2,128,64,2]{2,1,0,3:T(8,128)S(1)} %multiply_bitcast_fusion) | data formatting | bytes 262144 | tf_op jit(solution)/shard_map/while/body/eval_jaxpr/mul | solution.py:96
  73.2 94.4 %scatter_custom_fusion = f32[2,32768]{0,1:T(8,128)} fusion(s32[16384]{0:T(1024)S(1)} %reshape.558, f32[16384,2]{1,0:T(8,128)} %bitcast.299, f32[]{:T(128)} %constant.119.clone.1), kind=kCustom, calls=%fused_computation.37 | custom fusion | flops 32768 | bytes 262656
  167.5 27.8 %fusion.60 = (f32[1,1,128,128]{0,3,2,1:T(8,128)}, f32[1,1,128,128]{0,3,2,1:T(8,128)}, f32[1,1,128,128]{0,3,2,1:T(8,128)}, f32[1,1,128,128]{0,3,2,1:T(8,128)}) fusion(f32[2,2,128,128]{0,3,2,1:T(8,128)} %bitcast.298), kind=kLoop, calls=%fused_computation.153 | loop fusion | bytes 524288 | tf_op jit(solution)/shard_map/while/body/eval_jaxpr/slice | solution.py:74
  195.3 5.2 %copy.123 = f32[1,1,128,128]{3,2,1,0:T(8,128)S(1)} copy(f32[1,1,128,128]{0,3,2,1:T(8,128)} %get-tuple-element.218) | data formatting | bytes 131072
  200.6 5.2 %copy.122 = f32[1,1,128,128]{3,2,1,0:T(8,128)S(1)} copy(f32[1,1,128,128]{0,3,2,1:T(8,128)} %get-tuple-element.219) | data formatting | bytes 131072
  208.3 38.5 %while.40 = (s32[]{:T(128)}, f32[128,128]{0,1:T(8,128)S(1)}, f32[128,128]{0,1:T(8,128)S(1)}, f32[128,128]{1,0:T(8,128)S(1)}, f32[128,128]{1,0:T(8,128)S(1)}, /*index=5*/f32[128,128]{1,0:T(8,128)S(1)}, s32[]{:T(128)}) while((s32[]{:T(128)}, f32[128,128]{0,1:T(8,128)S(1)}, f32[128,128]{0,1:T(8,128)S(1)}, f32[128,128]{1,0:T(8,128)S(1)}, ...), condition=%wide.region_4.5_spmd.clone, body=%wide.region_3.4_spmd.clone.sunk | while | flops 151273472 | bytes 2162765 | solution.py:63
  247.6 5.2 %copy.124 = f32[1,1,128,128]{3,2,1,0:T(8,128)S(1)} copy(f32[1,1,128,128]{0,3,2,1:T(8,128)} %get-tuple-element.217) | data formatting | bytes 131072
  252.8 5.2 %copy.121 = f32[1,1,128,128]{3,2,1,0:T(8,128)S(1)} copy(f32[1,1,128,128]{0,3,2,1:T(8,128)} %get-tuple-element.220) | data formatting | bytes 131072
  258.1 0.9 multiply_reduce_fusion.1
  259.0 0.9 multiply_reduce_fusion.2
  261.1 38.5 %while.41 = (s32[]{:T(128)}, f32[128,128]{0,1:T(8,128)S(1)}, f32[128,128]{0,1:T(8,128)S(1)}, f32[128,128]{1,0:T(8,128)S(1)}, f32[128,128]{1,0:T(8,128)S(1)}, /*index=5*/f32[128,128]{1,0:T(8,128)S(1)}, s32[]{:T(128)}) while((s32[]{:T(128)}, f32[128,128]{0,1:T(8,128)S(1)}, f32[128,128]{0,1:T(8,128)S(1)}, f32[128,128]{1,0:T(8,128)S(1)}, ...), condition=%wide.region_8.9_spmd.clone, body=%wide.region_7.8_spmd.clone.sunk | while | flops 151273472 | bytes 2162765 | solution.py:63
  (416 shorter events, 92.5 us)
Async XLA Ops:
  0.0 247.0 %copy-start = (f32[1,128,128]{2,1,0:T(8,128)S(1)}, f32[1,128,128]{2,1,0:T(8,128)}, u32[]{:S(2)}) copy-start(f32[1,128,128]{2,1,0:T(8,128)} %param.13) | copy-start | bytes 196612
  0.0 60.6 %copy-start.2 = (s32[256]{0:T(256)S(1)}, s32[256]{0:T(256)}, u32[]{:S(2)}) copy-start(s32[256]{0:T(256)} %param.15) | copy-start | bytes 3076
  10.5 33.4 %all-to-all-start = ((f32[16,2,1,1024]{3,1,2,0:T(2,128)}), f32[16,2,1,1024]{3,1,2,0:T(2,128)S(1)}, u32[]{:S(2)}, u32[]{:S(2)}) async-start(f32[16,2,1,1024]{3,1,2,0:T(2,128)} %constant_dynamic-update-slice_fusion), calls=%async_computation | async-start | bytes 262144 | tf_op jit(solution)/shard_map/all_to_all | solution.py:153
  44.0 7.6 %collective-permute-start.1 = (f32[2,16,1024]{2,1,0:T(8,128)S(1)}, f32[2,16,1024]{2,1,0:T(8,128)S(1)}, u32[]{:S(2)}, u32[]{:S(2)}) collective-permute-start(f32[2,16,1024]{2,1,0:T(8,128)S(1)} %bitcast.300), channel_id=1, source_target_pairs={{16,0},{17,1},{18,2},{19,3},{20,4},{21,5},{22,6},{23,7},{24,8},{25... | collective-permute-start | bytes 393224 | tf_op jit(solution)/shard_map/ppermute | solution.py:27
  45.3 7.5 %collective-permute-start = (f32[2,16,1024]{2,1,0:T(8,128)S(1)}, f32[2,16,1024]{2,1,0:T(8,128)S(1)}, u32[]{:S(2)}, u32[]{:S(2)}) collective-permute-start(f32[2,16,1024]{2,1,0:T(8,128)S(1)} %bitcast.301), channel_id=1, source_target_pairs={{0,16},{1,17},{2,18},{3,19},{4,20},{5,21},{6,22},{7,23},{8,24},{9,... | collective-permute-start | bytes 393224 | tf_op jit(solution)/shard_map/ppermute | solution.py:25
  54.8 13.4 %all-to-all-start.1 = ((f32[2,16,1024]{2,0,1:T(2,128)}), f32[2,16,1024]{2,0,1:T(2,128)S(1)}, u32[]{:S(2)}, u32[]{:S(2)}) async-start(f32[2,16,1024]{2,0,1:T(2,128)} %copy.90), calls=%async_computation.1 | async-start | bytes 262144 | tf_op jit(solution)/shard_map/all_to_all | solution.py:161
  195.3 10.5 %copy-start.1 = (f32[2,128,128]{2,1,0:T(8,128)S(1)}, f32[2,128,128]{2,1,0:T(8,128)}, u32[]{:S(2)}) copy-start(f32[2,128,128]{2,1,0:T(8,128)} %param.12) | copy-start | bytes 393220
